TPU v7x, 32 devices: a whole 2x2x4 slice. The times are simulated.
32 devices in a mesh: wide: 8 (over y, x, core), narrow: 4 (over z).
Axes of the slice: x: 2, y: 2, z: 4, core: 2. Of those that a mesh axis runs over, the one named last changes fastest.
Arguments:
- amps: float32 [1, 16, 640, 640], P(None, 'wide', 'narrow'), may hold values from -6 to 6
- cycle: float32 [16, 640, 5120], P(None, 'wide', 'narrow'), may hold values from -0.25 to 0.25
- irrep_i: int32 [1], replicated, may hold values from 0 to 7
- irrep_k: int32 [16], replicated, may hold values from 0 to 7, as said below
- irrep_j: int32 [8], replicated, may hold values from 0 to 7, as said below
- irrep_v: int32 [640], replicated, may hold values from 0 to 7, as said below
Outputs:
- cycle_term: float32 [1, 8, 640, 640], P(None, 'wide', 'narrow')
Inputs may be any that keep to these rules, and one draw needn't show every extreme that they name: `irrep_k`: nondecreasing along the orbitals, the first 0 and the last 7. `irrep_j`: nondecreasing along the orbitals, the first 0 and the last 7. `irrep_v`: nondecreasing along the orbitals, the first 0 and the last 7.
All inputs are finite; a program needn't handle non-finite values.
Results may differ from a plain program's by a relative error of at most 0.000071.
Values sent between devices are 32-bit elements; how exact they have to be, the bound alone decides.
A program may use at most 64 MiB of HBM per device.

v0:
```python
import jax
import jax.numpy as jnp
from jax import lax
from jax.sharding import PartitionSpec as P


def per_device(amps, cycle, irrep_i, irrep_k, irrep_j, irrep_v):
    wide_pos = lax.axis_index("wide")
    narrow_pos = lax.axis_index("narrow")
    wide_count = lax.axis_size("wide")
    narrow_count = lax.axis_size("narrow")
    i_total = amps.shape[0]
    k_local = amps.shape[1]
    a_local = amps.shape[2]
    v_total = amps.shape[3]
    k_total = cycle.shape[0]
    c_local = cycle.shape[1]
    b_local = v_total // narrow_count
    j_total = cycle.shape[2] // b_local
    j_local = j_total // wide_count
    cycle_four = cycle.reshape(k_total, c_local, b_local, j_total)
    k_labels = lax.dynamic_slice_in_dim(irrep_k, wide_pos * k_local, k_local)
    a_labels = lax.dynamic_slice_in_dim(irrep_v, narrow_pos * a_local, a_local)
    allowed_in = (
        irrep_i[:, None, None, None]
        ^ k_labels[None, :, None, None]
        ^ a_labels[None, None, :, None]
        ^ irrep_v[None, None, None, :]
        == 0
    )
    masked = jnp.where(allowed_in, amps, jnp.zeros_like(amps))
    moved = lax.all_to_all(masked, "wide", split_axis=3, concat_axis=1, tiled=True)
    piece = lax.all_gather(moved, "narrow", axis=2, tiled=True)
    part_sum = jnp.einsum("ikac,kcbj->iajb", piece, cycle_four, precision=lax.Precision.HIGHEST)
    terms = part_sum.reshape(piece.shape[0], piece.shape[2], j_total * b_local)
    summed = lax.psum_scatter(terms, "wide", scatter_dimension=2, tiled=True)
    summed_four = summed.reshape(i_total, v_total, j_local, b_local)
    j_labels = lax.dynamic_slice_in_dim(irrep_j, wide_pos * j_local, j_local)
    b_labels = lax.dynamic_slice_in_dim(irrep_v, narrow_pos * b_local, b_local)
    allowed_out = (
        irrep_i[:, None, None, None]
        ^ irrep_v[None, :, None, None]
        ^ j_labels[None, None, :, None]
        ^ b_labels[None, None, None, :]
        == 0
    )
    result = jnp.where(allowed_out, summed_four, jnp.zeros_like(summed_four)).reshape(
        i_total, v_total, j_local * b_local
    )
    returned = lax.all_to_all(result, "narrow", split_axis=1, concat_axis=2, tiled=True)
    spread = returned.reshape(i_total, a_local, narrow_count, j_local, b_local)
    return jnp.transpose(spread, (0, 3, 1, 2, 4)).reshape(i_total, j_local, a_local, v_total)


def solution(mesh):
    placed = (P(None, "wide", "narrow", None), P(None, "wide", "narrow"), P(), P(), P(), P())
    return jax.shard_map(
        per_device,
        mesh=mesh,
        in_specs=placed,
        out_specs=P(None, "wide", "narrow", None),
        check_vma=False,
    )
```

profile of v0, /device:TPU:0, one launch (start us, length us, event | category | flops | bytes accessed | tf_op | source)
XLA Modules:
  0.0 275.7 jit_solution(13251704546821410816)
XLA Ops:
  7.2 2.5 copy.21
  9.7 0.8 dynamic_slice.11
  10.5 0.7 dynamic-slice_xor_fusion
  11.2 0.1 broadcast_xor_fusion
  11.3 2.5 compare_select_fusion
  13.8 23.1 %all_to_all.33 = f32[1,2,160,640]{2,1,0,3:T(2,128)S(1)} all-to-all(f32[1,2,160,640]{2,1,0,3:T(2,128)S(1)} %compare_select_fusion), channel_id=1, replica_groups=mesh['wide'=8,'narrow'=4] {'wide'}, dimensions={3} | all-to-all | bytes 1638400 | tf_op jit(solution)/shard_map/all_to_all | solution.py:32
  36.9 2.2 copy.22
  39.1 0.0 all-reduce.3.cloned.1.call-start
  39.1 9.9 %copy.24 = f32[16,80,1280]{1,2,0:T(8,128)} copy(f32[16,80,1280]{2,1,0:T(8,128)} %param.7) | data formatting | bytes 13107200 | tf_op args[1]
  49.1 87.6 %all-gather.2.cloned.1.call-done = f32[1,16,640,80]{3,1,0,2:T(8,128)} async-done(((f32[1,16,160,80]{3,1,0,2:T(8,128)}), f32[1,16,640,80]{3,1,0,2:T(8,128)}) %all-gather.2.cloned.1.call-update) | async-done | bytes 3276816 | tf_op jit(solution)/shard_map/all_gather | solution.py:33
  136.7 4.5 %copy.23 = f32[1,16,640,80]{2,3,1,0:T(8,128)S(1)} copy(f32[1,16,640,80]{3,1,0,2:T(8,128)} %all-gather.2.cloned.1.call-done) | data formatting | bytes 6553600 | tf_op jit(solution)/shard_map/all_gather | solution.py:33
  141.1 23.5 %fusion = f32[640,160,8,1]{0,1,3,2:T(8,128)S(1)} fusion(f32[16,80,160,8]{1,3,2,0:T(8,128)} %bitcast.27, f32[1,16,640,80]{2,3,1,0:T(8,128)S(1)} %copy.23), kind=kOutput, calls=%fused_computation | convolution fusion | flops 12582912000 | bytes 13107200 | tf_op jit(solution)/shard_map/ikac,kcbj->iajb/dot_general | solution.py:34
  164.6 8.5 %copy.26 = f32[1,640,1280]{1,0,2:T(1,128)} copy(f32[1,640,1280]{1,2,0:T(8,128)S(1)} %bitcast.30) | data formatting | bytes 6553600 | tf_op jit(solution)/shard_map/reshape | solution.py:35
  173.1 0.0 all-reduce.3.cloned.1.call-update
  173.1 0.6 copy-done.1
  173.8 0.7 dynamic_slice.10
  174.4 0.7 dynamic-slice
  175.8 0.7 xor_xor_fusion
  176.5 66.1 %all-reduce.3.cloned.1.call-done = f32[1,640,1280]{1,0,2:T(1,128)} async-done(((f32[1,640,1280]{1,0,2:T(1,128)}), f32[1,640,1280]{1,0,2:T(1,128)}) %all-reduce.3.cloned.1.call-update) | async-done | bytes 3276816
  242.6 1.5 compare_select_fusion.1
  244.1 1.8 copy.27
  245.8 21.5 %all_to_all.34 = f32[1,640,160]{2,0,1:T(1,128)S(1)} all-to-all(f32[1,640,160]{2,0,1:T(1,128)S(1)} %copy.27), channel_id=1, replica_groups=mesh['wide'=8,'narrow'=4] {'narrow'}, dimensions={1} | all-to-all | bytes 819200 | tf_op jit(solution)/shard_map/all_to_all | solution.py:50
  267.3 0.4 copy.28
  267.8 1.1 reshape_transpose_reshape.3
  (7 shorter events, 0.0 us)
Async XLA Ops:
  6.5 130.1 %all-gather.2.cloned.1.call-start = ((), (), s32[]{:S(2)}) async-start(), calls=%async_computation.2 | async-start | bytes 6553600 | tf_op jit(solution)/shard_map/all_gather | solution.py:33
  39.1 203.5 %all-reduce.3.cloned.1.call-start = ((), (), s32[]{:S(2)}) async-start(), calls=%async_computation.3 | async-start | bytes 6553600
  173.1 0.7 copy-start.1
  173.1 1.3 copy-start.2
  173.1 2.7 copy-start
Sparse Core Ops, SparseCore 0:
  39.2 97.4 all-gather.1
  173.3 69.2 all-reduce.2
where the time goes:
time: 276 us
  waiting for transfers between devices  154 us (56%)
  blocking collectives  44.7 us (16%)
  local copies, waits for them, and re-layouts  33.6 us (12%)
  matrix products  23.5 us (9%)
  between operations  14.8 us (5%)
  other arithmetic  5.46 us (2%)
    all_gather x1, waiting for transfers between devices, per_device(): piece = lax.all_gather(moved, 'narrow', axis=2, tiled=True)  87.6 us
    unnamed x3, waiting for transfers between devices  66.1 us
    dot_general x1, matrix products, per_device(): jnp.einsum('ikac,kcbj->iajb', piece, cycle_four, precision=lax.Precision....  23.5 us
    all_to_all x1, blocking collectives, per_device(): lax.all_to_all(masked, 'wide', split_axis=3, concat_axis=1, tiled=True)  23.1 us
    all_to_all x1, blocking collectives, per_device(): lax.all_to_all(result, 'narrow', split_axis=1, concat_axis=2, tiled=True)  21.5 us
    unnamed x9, local copies, waits for them, and re-layouts  13.7 us
    reshape x1, local copies, waits for them, and re-layouts, per_device(): terms = part_sum.reshape(piece.shape[0], piece.shape[2], j_total * b_local)  8.52 us
  transfers between devices with their start and end apart: 2, of which 2 were waited for; matrix products, arithmetic and copies ran while one was open for 4% of the time, Pallas kernels for 0%

commit v1 on v0

--- a/solution.py
+++ b/solution.py
@@ -47,7 +47,12 @@
     result = jnp.where(allowed_out, summed_four, jnp.zeros_like(summed_four)).reshape(
         i_total, v_total, j_local * b_local
     )
-    returned = lax.all_to_all(result, "narrow", split_axis=1, concat_axis=2, tiled=True)
+    returned = jnp.concatenate(
+        lax.all_to_all(
+            jnp.stack(jnp.split(result, lax.axis_size("narrow"), axis=1)), "narrow", 0, 0
+        ),
+        axis=2,
+    )
     spread = returned.reshape(i_total, a_local, narrow_count, j_local, b_local)
     return jnp.transpose(spread, (0, 3, 1, 2, 4)).reshape(i_total, j_local, a_local, v_total)
 

time: 276 us -> 242 us (0.88)
  waiting for transfers between devices: 154 us -> 131 us
  local copies, waits for them, and re-layouts: 33.6 us -> 22.3 us
    unnamed x3 -> x2, waiting for transfers between devices: 66.1 us -> 0.03 us
    reduce_scatter x0 -> x1, waiting for transfers between devices: none -> 43.4 us  [per_device(): summed = lax.psum_scatter(terms, 'wide', scatter_dimension=2, tiled=True)]
    reshape x1 -> x0, local copies, waits for them, and re-layouts: 8.52 us -> none  [per_device(): terms = part_sum.reshape(piece.shape[0], piece.shape[2], j_total * b_local)]
    unnamed x9 -> x6, local copies, waits for them, and re-layouts: 13.7 us -> 13.1 us
  transfers between devices with their start and end apart: 2 -> 2, of which waited for: 2 -> 2; matrix products, arithmetic and copies ran while one was open for 4% -> 5% of each run, Pallas kernels for 0% -> 0%
where the time goes in v1:
time: 242 us; the launch traced here: 241 us
  waiting for transfers between devices  131 us (54%)
  blocking collectives  44.8 us (19%)
  matrix products  23.8 us (10%)
  local copies, waits for them, and re-layouts  22.3 us (9%)
  between operations  14.1 us (6%)
  other arithmetic  5.13 us (2%)
    all_gather x1, waiting for transfers between devices, per_device(): piece = lax.all_gather(moved, 'narrow', axis=2, tiled=True)  87.6 us
    reduce_scatter x1, waiting for transfers between devices, per_device(): summed = lax.psum_scatter(terms, 'wide', scatter_dimension=2, tiled=True)  43.4 us
    dot_general x1, matrix products, per_device(): jnp.einsum('ikac,kcbj->iajb', piece, cycle_four, precision=lax.Precision....  23.8 us
    all_to_all x1, blocking collectives, per_device(): lax.all_to_all(masked, 'wide', split_axis=3, concat_axis=1, tiled=True)  23.1 us
    all_to_all x1, blocking collectives, per_device(): lax.all_to_all(jnp.stack(jnp.split(result, lax.axis_size('narrow'), axis=...  21.7 us
    unnamed x6, local copies, waits for them, and re-layouts  13.1 us
  transfers between devices with their start and end apart: 2, of which 2 were waited for; matrix products, arithmetic and copies ran while one was open for 5% of the time, Pallas kernels for 0%

profile of v1, /device:TPU:0, one launch (start us, length us, event | category | flops | bytes accessed | tf_op | source)
XLA Modules:
  0.0 241.2 jit_solution(17728014064904734612)
XLA Ops:
  6.5 0.0 all-gather.2.cloned.1.call-start
  7.2 2.5 %copy.14 = f32[1,2,160,640]{2,1,0,3:T(2,128)S(1)} copy(f32[1,2,160,640]{3,2,1,0:T(8,128)} %param.6) | data formatting | bytes 1638400 | tf_op args[0]
  9.7 0.8 dynamic_slice.11
  10.5 0.7 dynamic-slice_xor_fusion
  11.2 0.1 broadcast_xor_fusion
  11.3 2.5 %compare_select_fusion = f32[1,2,160,640]{2,1,0,3:T(2,128)S(1)} fusion(f32[1,2,160,640]{2,1,0,3:T(2,128)S(1)} %copy.14, s32[2,160]{1,0:T(2,128)S(1)} %broadcast_xor_fusion, s32[640]{0:T(1024)} %param.11), kind=kLoop, calls=%fused_computation.3 | loop fusion | flops 614400 | bytes 1642240 | tf_op jit(solution)/shard_map/jit(_where)/select_n | solution.py:31
  13.8 23.1 %all_to_all.23 = f32[1,2,160,640]{2,1,0,3:T(2,128)S(1)} all-to-all(f32[1,2,160,640]{2,1,0,3:T(2,128)S(1)} %compare_select_fusion), channel_id=1, replica_groups=mesh['wide'=8,'narrow'=4] {'wide'}, dimensions={3} | all-to-all | bytes 1638400 | tf_op jit(solution)/shard_map/all_to_all | solution.py:32
  36.9 2.2 copy.15
  39.0 0.0 all-gather.2.cloned.1.call-update
  39.1 0.0 reduce-scatter.2.cloned.1.call-start
  39.1 9.9 %copy.17 = f32[16,80,1280]{1,2,0:T(8,128)} copy(f32[16,80,1280]{2,1,0:T(8,128)} %param.7) | data formatting | bytes 13107200 | tf_op args[1]
  49.1 87.6 %all-gather.2.cloned.1.call-done = f32[1,16,640,80]{3,1,0,2:T(8,128)} async-done(((f32[1,16,160,80]{3,1,0,2:T(8,128)}), f32[1,16,640,80]{3,1,0,2:T(8,128)}) %all-gather.2.cloned.1.call-update) | async-done | bytes 3276816 | tf_op jit(solution)/shard_map/all_gather | solution.py:33
  136.7 4.5 %copy.16 = f32[1,16,640,80]{2,3,1,0:T(8,128)S(1)} copy(f32[1,16,640,80]{3,1,0,2:T(8,128)} %all-gather.2.cloned.1.call-done) | data formatting | bytes 6553600 | tf_op jit(solution)/shard_map/all_gather | solution.py:33
  141.1 23.8 %fusion = f32[640,160,8,1]{0,1,3,2:T(8,128)} fusion(f32[16,80,160,8]{1,3,2,0:T(8,128)} %bitcast.34, f32[1,16,640,80]{2,3,1,0:T(8,128)S(1)} %copy.16), kind=kOutput, calls=%fused_computation | convolution fusion | flops 12582912000 | bytes 13107200 | tf_op jit(solution)/shard_map/ikac,kcbj->iajb/dot_general | solution.py:34
  164.9 0.0 reduce-scatter.2.cloned.1.call-update
  165.0 0.6 copy-done.1
  165.6 0.7 dynamic_slice.10
  166.3 0.0 copy-done
  166.3 0.7 xor_xor_fusion
  167.0 43.4 %reduce-scatter.2.cloned.1.call-done = f32[1,640,160]{1,2,0:T(8,128)} async-done(((f32[1,640,1280]{1,2,0:T(8,128)}), f32[1,640,160]{1,2,0:T(8,128)}) %reduce-scatter.2.cloned.1.call-update) | async-done | bytes 409616 | tf_op jit(solution)/shard_map/reduce_scatter | solution.py:36
  210.4 1.1 fusion.3
  211.5 0.2 slice_bitcast_fusion.3
  211.7 21.7 %all_to_all.24 = f32[4,1,160,160]{2,3,1,0:T(8,128)S(1)} all-to-all(f32[4,1,160,160]{2,3,1,0:T(8,128)S(1)} %pad_maximum_fusion), channel_id=1, replica_groups=mesh['wide'=8,'narrow'=4] {'narrow'}, dimensions={0} | all-to-all | bytes 819200 | tf_op jit(solution)/shard_map/all_to_all | solution.py:51
  233.4 1.0 copy.21
  (3 shorter events, 0.0 us)
Async XLA Ops:
  6.5 130.1 %all-gather.2.cloned.1.call-start = ((), (), s32[]{:S(2)}) async-start(), calls=%async_computation.3 | async-start | bytes 6553600 | tf_op jit(solution)/shard_map/all_gather | solution.py:33
  39.1 171.3 %reduce-scatter.2.cloned.1.call-start = ((), (), s32[]{:S(2)}) async-start(), calls=%async_computation.4 | async-start | bytes 3686400 | tf_op jit(solution)/shard_map/reduce_scatter | solution.py:36
  164.9 0.7 copy-start.1
  164.9 1.3 copy-start
Sparse Core Ops, SparseCore 0:
  39.2 97.4 all-gather.1
  165.1 45.2 reduce-scatter.1
